TPU v7x, 32 devices: a whole 2x2x4 slice. The times are simulated.
32 devices in a mesh: fsdp: 16 (over z, y, core), expert: 2 (over x).
Axes of the slice: x: 2, y: 2, z: 4, core: 2. Of those that a mesh axis runs over, the one named last changes fastest.
Arguments:
- tokens: bfloat16 [8192, 1024], P(('fsdp', 'expert')), may hold values from -6 to 6
- query_weight: bfloat16 [1024, 1024], P(('fsdp', 'expert')), may hold values from -0.1875 to 0.1875
- key_projection: bfloat16 [1024, 512], P(('fsdp', 'expert')), may hold values from -0.1875 to 0.1875
- value_projection: bfloat16 [1024, 512], P(('fsdp', 'expert')), may hold values from -0.1875 to 0.1875
- output_weight: bfloat16 [1024, 1024], P(('fsdp', 'expert')), may hold values from -0.75 to 0.75
- router_weight: bfloat16 [1024, 32], P(('fsdp', 'expert')), may hold values from -0.375 to 0.375
- attn_gain: bfloat16 [1024], P(('fsdp', 'expert')), may hold values from 0.5 to 1.5
- ffn_gain: bfloat16 [1024], P(('fsdp', 'expert')), may hold values from 0.5 to 1.5
- gate_weight: bfloat16 [32, 1024, 512], P('expert', 'fsdp'), may hold values from -0.1875 to 0.1875
- up_weight: bfloat16 [32, 1024, 512], P('expert', 'fsdp'), may hold values from -0.1875 to 0.1875
- down_weight: bfloat16 [32, 512, 1024], P('expert', 'fsdp'), may hold values from -0.75 to 0.75
- lengths: int32 [32, 2, 4], P(('fsdp', 'expert')), may hold values from 1 to 64, 128 in all within a row
- routes: int32 [8192, 8], P(('fsdp', 'expert')), may hold values from 0 to 31, all different within a row; in each aligned block of 128 rows (0 to 127, 128 to 255, ...) at most 40 rows name the same one
- cotangent: bfloat16 [8192, 1024], P(('fsdp', 'expert')), may hold values from -6 to 6
Outputs:
- layer_out: bfloat16 [8192, 1024], P(('fsdp', 'expert'))
- grad_tokens: float32 [8192, 1024], P(('fsdp', 'expert'))
- grad_query: float32 [1024, 1024], P(('fsdp', 'expert'))
- grad_key: float32 [1024, 512], P(('fsdp', 'expert'))
- grad_value: float32 [1024, 512], P(('fsdp', 'expert'))
- grad_output: float32 [1024, 1024], P(('fsdp', 'expert'))
- grad_router: float32 [1024, 32], P(('fsdp', 'expert'))
- grad_attn_gain: float32 [1024], P(('fsdp', 'expert'))
- grad_ffn_gain: float32 [1024], P(('fsdp', 'expert'))
- grad_gate: float32 [32, 1024, 512], P('expert', 'fsdp')
- grad_up: float32 [32, 1024, 512], P('expert', 'fsdp')
- grad_down: float32 [32, 512, 1024], P('expert', 'fsdp')
Inputs may be any that keep to these rules, and one draw needn't show every extreme that they name: Each micro-batch of each device holds 4 sequences whose lengths sum to 128; the longest is exactly 64 tokens in every micro-batch. `routes`: the 8 experts of a row differ; in each aligned block of 128 rows (one micro-batch of one device) no expert is named by more than 40 rows, a bound that some block reaches.
All inputs are finite; a program needn't handle non-finite values.
Results may differ from a plain program's by a relative error of at most 0.015.
The roundings to bfloat16 on the way count: a program that leaves them out, or rounds other values in their place, can miss the bound.
Values may be sent and summed in bfloat16 or wider, within the bound.
No kernel may reach another device: no remote copies, remote signals or barrier semaphores. Data moves between devices by JAX's collectives and lax.ppermute only.
A program may use at most 256 MiB of HBM per device.

v0:
```python
import jax
import jax.numpy as jnp
from jax import lax
from jax.sharding import PartitionSpec as P

MODEL_WIDTH = 1024
QUERY_HEADS = 16
KEY_VALUE_HEADS = 8
HEAD_SIZE = 64
EXPERTS = 32
DEVICE_TOKENS = 128
MB = 2
CAP = 40
ROWS = MB * DEVICE_TOKENS
SLOTS = MB * CAP
Q_COLS = QUERY_HEADS * HEAD_SIZE
KV_COLS = KEY_VALUE_HEADS * HEAD_SIZE
QKV_COLS = Q_COLS + 2 * KV_COLS
SMALL_COLS = 128
EPS = 1e-06
THETA = 10000.0
SCALE = 0.125
HIGH = lax.Precision.HIGHEST
BOTH = ("fsdp", "expert")
F32 = jnp.float32
BF16 = jnp.bfloat16


def mm(spec, a, b):
    return jnp.einsum(spec, a, b, preferred_element_type=F32)


def sequence_layout(seq_lengths, row_number):
    row_index = jnp.arange(row_number, dtype=jnp.int32)
    seq_ends = jnp.cumsum(seq_lengths)
    starts = seq_ends - seq_lengths
    member = (
        (row_index[:, None] >= starts[None, :]) & (row_index[:, None] < seq_ends[None, :])
    ).astype(jnp.int32)
    labels = jnp.arange(seq_lengths.shape[0], dtype=jnp.int32)
    segment = jnp.sum(member * labels[None, :], axis=1)
    offset = jnp.sum(member * starts[None, :], axis=1)
    return (segment, row_index - offset)


def rotary_tables(token_positions):
    half_width = HEAD_SIZE // 2
    frequency = THETA ** (-2.0 * jnp.arange(half_width, dtype=F32) / HEAD_SIZE)
    angles = token_positions.astype(F32)[:, None] * frequency[None, :]
    return (jnp.cos(angles)[:, None, :], jnp.sin(angles)[:, None, :])


def rotary_apply(values, cosine, sine_part):
    half_width = HEAD_SIZE // 2
    first_half = values[..., :half_width]
    second_half = values[..., half_width:]
    return jnp.concatenate(
        [
            first_half * cosine - second_half * sine_part,
            second_half * cosine + first_half * sine_part,
        ],
        axis=-1,
    )


def rms_scale(values):
    return lax.rsqrt(jnp.mean(values * values, axis=1, keepdims=True) + EPS)


def norm_back(grad_normed, gain_vec, plain_part, scale_part):
    grad_gain = jnp.sum(grad_normed * plain_part, axis=0)
    shaped = grad_normed * gain_vec[None, :]
    grad_input = scale_part * (
        shaped - plain_part * jnp.mean(shaped * plain_part, axis=1, keepdims=True)
    )
    return (grad_input, grad_gain)


def fsdp_groups(local_experts):
    size = lax.axis_size("fsdp")
    runs = size // local_experts
    if runs == 1:
        return (None, None)
    inner = [[s * local_experts + j for j in range(local_experts)] for s in range(runs)]
    cross = [[s * local_experts + j for s in range(runs)] for j in range(local_experts)]
    return (inner, cross)


def weight_to_expert(weight, inner, cross):
    part = lax.all_to_all(
        weight, "fsdp", split_axis=0, concat_axis=1, axis_index_groups=inner, tiled=True
    )[0]
    if cross is not None:
        part = lax.all_gather(part, "fsdp", axis=0, axis_index_groups=cross, tiled=True)
    return part


def grad_to_owners(grad, inner, cross):
    if cross is not None:
        grad = lax.psum_scatter(
            grad, "fsdp", scatter_dimension=0, axis_index_groups=cross, tiled=True
        )
    return lax.all_to_all(
        grad.astype(BF16)[None],
        "fsdp",
        split_axis=1,
        concat_axis=0,
        axis_index_groups=inner,
        tiled=True,
    ).astype(F32)


def exchange(rows, local_experts, inner):
    if inner is None:
        return lax.all_to_all(rows, BOTH, split_axis=0, concat_axis=0, tiled=True)
    groups = EXPERTS // local_experts
    shaped = rows.reshape((local_experts, groups) + rows.shape[1:])
    shaped = lax.all_to_all(
        shaped, "fsdp", split_axis=0, concat_axis=0, axis_index_groups=inner, tiled=True
    )
    shaped = lax.all_to_all(shaped, "expert", split_axis=1, concat_axis=1, tiled=True)
    return shaped.reshape(rows.shape)


def sum_to_owners(grad):
    devices = lax.axis_size(BOTH)
    parts = grad.reshape(devices, grad.shape[0] // devices, grad.shape[1])
    parts = lax.all_to_all(parts, BOTH, split_axis=0, concat_axis=0, tiled=True)
    return jnp.sum(parts.astype(F32), axis=0)


def per_device(
    tokens,
    query_weight,
    key_projection,
    value_projection,
    output_weight,
    router_weight,
    attn_gain,
    ffn_gain,
    gate_weight,
    up_weight,
    down_weight,
    lengths,
    routes,
    cotangent,
):
    local_experts = gate_weight.shape[0]
    groups = EXPERTS // local_experts
    inner, cross = fsdp_groups(local_experts)
    heads = QUERY_HEADS // KEY_VALUE_HEADS
    small = jnp.concatenate(
        [
            router_weight,
            attn_gain[:, None],
            ffn_gain[:, None],
            jnp.zeros((router_weight.shape[0], SMALL_COLS - EXPERTS - 2), BF16),
        ],
        axis=1,
    )
    packed = jnp.concatenate(
        [query_weight, key_projection, value_projection, output_weight, small], axis=1
    )
    full = lax.all_gather(packed, BOTH, axis=0, tiled=True)
    qkv_full = full[:, :QKV_COLS]
    o_full = full[:, QKV_COLS : QKV_COLS + MODEL_WIDTH]
    small_full = full[:, QKV_COLS + MODEL_WIDTH :]
    r_full = small_full[:, :EXPERTS]
    gain_one = small_full[:, EXPERTS].astype(F32)
    gain_two = small_full[:, EXPERTS + 1].astype(F32)
    gate_full = weight_to_expert(gate_weight, inner, cross)
    up_full = weight_to_expert(up_weight, inner, cross)
    down_full = weight_to_expert(down_weight, inner, cross)
    plain_in = tokens.astype(F32)
    grad_out = cotangent.astype(F32)
    layouts = [sequence_layout(lengths[0, b], DEVICE_TOKENS) for b in range(MB)]
    segment = jnp.stack([s for s, _ in layouts])
    cosine, sine = rotary_tables(jnp.concatenate([p for _, p in layouts]))
    row_index = jnp.arange(DEVICE_TOKENS, dtype=jnp.int32)
    allowed = (segment[:, :, None] == segment[:, None, :]) & (
        row_index[:, None] >= row_index[None, :]
    )[None]
    local = jnp.arange(EXPERTS, dtype=jnp.int32)
    named = local % groups * local_experts + local // groups
    hits = jnp.any(routes[:, :, None] == named[None, None, :], axis=1)
    all_rows = jnp.arange(ROWS, dtype=jnp.int32)
    below = (all_rows[:, None] > all_rows[None, :]).astype(BF16)
    rank = mm("ts,se->te", below, hits.astype(BF16)).astype(jnp.int32)
    rank = jnp.where(hits, rank, -1)
    slot_id = jnp.arange(SLOTS, dtype=jnp.int32)
    place = rank.T[:, None, :] == slot_id[None, :, None]
    place_rows = place.astype(BF16).reshape(EXPERTS * SLOTS, ROWS)
    scale_one = rms_scale(plain_in)
    plain_one = plain_in * scale_one
    attention_input = (plain_one * gain_one[None, :]).astype(BF16)
    qkv = mm("td,de->te", attention_input, qkv_full)
    query = (
        rotary_apply(qkv[:, :Q_COLS].reshape(ROWS, QUERY_HEADS, HEAD_SIZE), cosine, sine)
        .astype(BF16)
        .reshape(MB, DEVICE_TOKENS, KEY_VALUE_HEADS, heads, HEAD_SIZE)
    )
    key = (
        rotary_apply(
            qkv[:, Q_COLS : Q_COLS + KV_COLS].reshape(ROWS, KEY_VALUE_HEADS, HEAD_SIZE),
            cosine,
            sine,
        )
        .astype(BF16)
        .reshape(MB, DEVICE_TOKENS, KEY_VALUE_HEADS, HEAD_SIZE)
    )
    value = (
        qkv[:, Q_COLS + KV_COLS :]
        .astype(BF16)
        .reshape(MB, DEVICE_TOKENS, KEY_VALUE_HEADS, HEAD_SIZE)
    )
    scores = mm("bqgrd,bkgd->bgrqk", query, key) * SCALE
    scores = jnp.where(allowed[:, None, None], scores, -1e30)
    exp_scores = jnp.exp(scores - jnp.max(scores, axis=-1, keepdims=True))
    probs = exp_scores / jnp.sum(exp_scores, axis=-1, keepdims=True)
    probs_low = probs.astype(BF16)
    mixed = mm("bgrqk,bkgd->bqgrd", probs_low, value).reshape(ROWS, Q_COLS).astype(BF16)
    middle = plain_in + mm("te,ed->td", mixed, o_full)
    scale_two = rms_scale(middle)
    plain_two = middle * scale_two
    ffn_in = (plain_two * gain_two[None, :]).astype(BF16)
    dispatch = mm("st,td->sd", place_rows, ffn_in).astype(BF16)
    received = exchange(
        dispatch.reshape(EXPERTS, SLOTS, MODEL_WIDTH), local_experts, inner
    ).reshape(EXPERTS * SLOTS, MODEL_WIDTH)
    logits = mm("td,de->te", ffn_in, r_full)
    logits = logits.reshape(ROWS, groups, local_experts).swapaxes(1, 2).reshape(ROWS, EXPERTS)
    logits = jnp.where(hits, logits, -jnp.inf)
    exp_logits = jnp.exp(logits - jnp.max(logits, axis=1, keepdims=True))
    gates = exp_logits / jnp.sum(exp_logits, axis=1, keepdims=True)
    slot_gates = jnp.sum(jnp.where(place, gates.T[:, None, :], 0.0), axis=2)
    cot_rows = mm("st,td->sd", place_rows, cotangent).reshape(EXPERTS, SLOTS, MODEL_WIDTH)
    grad_recv = exchange(
        (slot_gates[:, :, None] * cot_rows).astype(BF16), local_experts, inner
    ).reshape(EXPERTS * SLOTS, MODEL_WIDTH)
    gate_act = mm("sd,dh->sh", received, gate_full)
    up_act = mm("sd,dh->sh", received, up_full)
    sigmoid_g = jax.nn.sigmoid(gate_act)
    silu_gate = gate_act * sigmoid_g
    hidden = (silu_gate * up_act).astype(BF16)
    produced = mm("sh,hd->sd", hidden, down_full).astype(BF16)
    returned = exchange(
        produced.reshape(EXPERTS, SLOTS, MODEL_WIDTH), local_experts, inner
    ).reshape(EXPERTS * SLOTS, MODEL_WIDTH)
    grad_hidden = mm("sd,hd->sh", grad_recv, down_full)
    grad_gact = (grad_hidden * up_act * sigmoid_g * (1.0 + gate_act * (1.0 - sigmoid_g))).astype(
        BF16
    )
    grad_uact = (grad_hidden * silu_gate).astype(BF16)
    grad_inputs = (
        mm("sh,dh->sd", grad_gact, gate_full) + mm("sh,dh->sd", grad_uact, up_full)
    ).astype(BF16)
    grad_back = exchange(
        grad_inputs.reshape(EXPERTS, SLOTS, MODEL_WIDTH), local_experts, inner
    ).reshape(EXPERTS * SLOTS, MODEL_WIDTH)
    grad_down = grad_to_owners(mm("sh,sd->hd", hidden, grad_recv), inner, cross)
    grad_gate = grad_to_owners(mm("sd,sh->dh", received, grad_gact), inner, cross)
    grad_up = grad_to_owners(mm("sd,sh->dh", received, grad_uact), inner, cross)
    slot_column = slot_gates.reshape(EXPERTS * SLOTS, 1)
    part_one = slot_column.astype(BF16)
    rest = slot_column - part_one.astype(F32)
    part_two = rest.astype(BF16)
    part_three = (rest - part_two.astype(F32)).astype(BF16)
    combined = (
        mm("st,sd->td", place_rows * part_three, returned)
        + mm("st,sd->td", place_rows * part_two, returned)
        + mm("st,sd->td", place_rows * part_one, returned)
    )
    layer_out = (middle + combined).astype(BF16)
    products = mm("sd,td->st", returned, cotangent).reshape(EXPERTS, SLOTS, ROWS)
    grad_gates = jnp.sum(jnp.where(place, products, 0.0), axis=1).T
    grad_logits = gates * (grad_gates - jnp.sum(gates * grad_gates, axis=1, keepdims=True))
    grad_logits = (
        grad_logits.reshape(ROWS, local_experts, groups).swapaxes(1, 2).reshape(ROWS, EXPERTS)
    )
    grad_router = jnp.dot(ffn_in.astype(F32).T, grad_logits, precision=HIGH)
    grad_ffn_in = jnp.dot(grad_logits, r_full.astype(F32).T, precision=HIGH)
    grad_ffn_in = grad_ffn_in + mm("st,sd->td", place_rows, grad_back)
    grad_middle, grad_gain_two = norm_back(grad_ffn_in, gain_two, plain_two, scale_two)
    grad_middle = grad_middle + grad_out
    grad_attn = grad_middle.astype(BF16)
    grad_o = sum_to_owners(mm("te,td->ed", mixed, grad_attn).astype(BF16))
    grad_mix = (
        mm("td,ed->te", grad_attn, o_full)
        .astype(BF16)
        .reshape(MB, DEVICE_TOKENS, KEY_VALUE_HEADS, heads, HEAD_SIZE)
    )
    grad_value = mm("bgrqk,bqgrd->bkgd", probs_low, grad_mix).astype(BF16).reshape(ROWS, KV_COLS)
    grad_probs = mm("bqgrd,bkgd->bgrqk", grad_mix, value)
    row_inner = jnp.sum(probs * grad_probs, axis=-1, keepdims=True)
    grad_scores = (probs * (grad_probs - row_inner)).astype(BF16)
    grad_query = mm("bgrqk,bkgd->bqgrd", grad_scores, key) * SCALE
    grad_query = (
        rotary_apply(grad_query.reshape(ROWS, QUERY_HEADS, HEAD_SIZE), cosine, -sine)
        .astype(BF16)
        .reshape(ROWS, Q_COLS)
    )
    grad_key = mm("bgrqk,bqgrd->bkgd", grad_scores, query) * SCALE
    grad_key = (
        rotary_apply(grad_key.reshape(ROWS, KEY_VALUE_HEADS, HEAD_SIZE), cosine, -sine)
        .astype(BF16)
        .reshape(ROWS, KV_COLS)
    )
    grad_qkv = jnp.concatenate([grad_query, grad_key, grad_value], axis=1)
    grad_qkv_w = mm("td,te->de", attention_input, grad_qkv).astype(BF16)
    grad_attn_in = mm("te,de->td", grad_qkv, qkv_full)
    grad_plain, grad_gain_one = norm_back(grad_attn_in, gain_one, plain_one, scale_one)
    small_grads = jnp.concatenate(
        [
            grad_router,
            grad_gain_one[:, None],
            grad_gain_two[:, None],
            jnp.zeros((MODEL_WIDTH, SMALL_COLS // 2 - EXPERTS - 2), F32),
        ],
        axis=1,
    )
    small_high = small_grads.astype(BF16)
    small_low = (small_grads - small_high.astype(F32)).astype(BF16)
    owned = sum_to_owners(jnp.concatenate([grad_qkv_w, small_high, small_low], axis=1))
    small_owned = (
        owned[:, QKV_COLS : QKV_COLS + SMALL_COLS // 2] + owned[:, QKV_COLS + SMALL_COLS // 2 :]
    )
    grad_qkv_w = owned[:, :QKV_COLS]
    return (
        layer_out,
        grad_plain + grad_middle,
        grad_qkv_w[:, :Q_COLS],
        grad_qkv_w[:, Q_COLS : Q_COLS + KV_COLS],
        grad_qkv_w[:, Q_COLS + KV_COLS :],
        grad_o,
        small_owned[:, :EXPERTS],
        small_owned[:, EXPERTS],
        small_owned[:, EXPERTS + 1],
        grad_gate,
        grad_up,
        grad_down,
    )


def solution(mesh):
    in_specs = (
        P(("fsdp", "expert"), None),
        P(("fsdp", "expert"), None),
        P(("fsdp", "expert"), None),
        P(("fsdp", "expert"), None),
        P(("fsdp", "expert"), None),
        P(("fsdp", "expert"), None),
        P(("fsdp", "expert")),
        P(("fsdp", "expert")),
        P("expert", "fsdp", None),
        P("expert", "fsdp", None),
        P("expert", "fsdp", None),
        P(("fsdp", "expert"), None, None),
        P(("fsdp", "expert"), None),
        P(("fsdp", "expert"), None),
    )
    out_specs = (
        P(("fsdp", "expert"), None),
        P(("fsdp", "expert"), None),
        P(("fsdp", "expert"), None),
        P(("fsdp", "expert"), None),
        P(("fsdp", "expert"), None),
        P(("fsdp", "expert"), None),
        P(("fsdp", "expert"), None),
        P(("fsdp", "expert")),
        P(("fsdp", "expert")),
        P("expert", "fsdp", None),
        P("expert", "fsdp", None),
        P("expert", "fsdp", None),
    )
    return jax.shard_map(
        per_device, mesh=mesh, in_specs=in_specs, out_specs=out_specs, check_vma=False
    )
```

profile of v0, /device:TPU:0, one launch (start us, length us, event | category | flops | bytes accessed | tf_op | source)
XLA Modules:
  0.0 914.2 jit_solution(18132010783329984123)
XLA Ops:
  10.5 7.4 all-to-all-start.1
  19.5 25.6 %all-to-all-done.1 = bf16[16,64,512]{2,1,0:T(8,128)(2,1)S(1)} async-done(((bf16[16,64,512]{2,1,0:T(8,128)(2,1)}), bf16[16,64,512]{2,1,0:T(8,128)(2,1)S(1)}, u32[]{:S(2)}, u32[]{:S(2)}) %all-to-all-start.1) | async-done | bytes 1048608 | tf_op jit(solution)/shard_map/all_to_all | solution.py:90
  45.1 6.8 all-to-all-start.2
  52.9 49.8 %all-gather.2.cloned.1.call-done = bf16[1024,3200]{1,0:T(8,128)(2,1)} async-done(((bf16[32,3200]{1,0:T(8,128)(2,1)}), bf16[1024,3200]{1,0:T(8,128)(2,1)}) %all-gather.2.cloned.1.call-update) | async-done | bytes 6553616 | tf_op jit(solution)/shard_map/all_gather | solution.py:164
  126.8 11.0 %all-to-all-done.3 = bf16[16,32,1024]{2,1,0:T(8,128)(2,1)} async-done(((bf16[16,32,1024]{2,1,0:T(8,128)(2,1)}), bf16[16,32,1024]{2,1,0:T(8,128)(2,1)}, u32[]{:S(2)}, u32[]{:S(2)}) %all-to-all-start.3) | async-done | bytes 1048608 | tf_op jit(solution)/shard_map/all_to_all | solution.py:90
  137.8 6.5 all-to-all-start
  149.6 110.8 %all-to-all-done = bf16[32,80,1024]{2,1,0:T(8,128)(2,1)} async-done(((bf16[32,80,1024]{2,1,0:T(8,128)(2,1)}), bf16[32,80,1024]{2,1,0:T(8,128)(2,1)}, u32[]{:S(2)}, u32[]{:S(2)}) %all-to-all-start) | async-done | bytes 5242912 | tf_op jit(solution)/shard_map/all_to_all | solution.py:115
  265.3 8.1 fusion.120
  273.4 7.1 fusion.119
  280.6 100.8 %all-to-all-done.5 = bf16[32,80,1024]{2,1,0:T(8,128)(2,1)} async-done(((bf16[32,80,1024]{2,1,0:T(8,128)(2,1)}), bf16[32,80,1024]{2,1,0:T(8,128)(2,1)}, u32[]{:S(2)}, u32[]{:S(2)}) %all-to-all-start.5) | async-done | bytes 5242912 | tf_op jit(solution)/shard_map/all_to_all | solution.py:115
  381.4 12.0 %multiply_convert_fusion.1 = (bf16[2560,512]{1,0:T(8,128)(2,1)}, bf16[2560,512]{1,0:T(8,128)(2,1)S(1)}, bf16[2560,512]{1,0:T(8,128)(2,1)}) fusion(f32[2560,512]{1,0:T(8,128)} %fusion.119, f32[2560,512]{1,0:T(8,128)} %fusion.120, bf16[2560,1024]{1,0:T(8,128)(2,1)} %bitcast.37, bf16[512,1024]{1,0:T(8,128)(2,1)} %bitcast.26), kind=kOutput, calls=%fused_computation.6 | convolution fusion | flops 2704015360 | bytes 24641536 | tf_op jit(solution)/shard_map/sd,hd->sh/dot_general | solution.py:30
  393.4 6.3 fusion.22
  401.9 8.0 reduce.10
  417.4 6.2 fusion.23
  425.3 8.0 reduce.11
  440.3 7.2 all-to-all-start.10
  447.5 7.2 convolution_convert_fusion.1
  454.8 15.6 %all-to-all-done.10 = bf16[16,2,16384]{2,1,0:T(2,128)(2,1)S(1)} async-done(((bf16[16,2,16384]{2,1,0:T(2,128)(2,1)}), bf16[16,2,16384]{2,1,0:T(2,128)(2,1)S(1)}, u32[]{:S(2)}, u32[]{:S(2)}) %all-to-all-start.10) | async-done | bytes 1048608 | tf_op jit(solution)/shard_map/all_to_all | solution.py:103
  471.4 6.9 all-to-all-start.4
  478.3 5.0 fusion.121
  483.3 6.1 add_convert_fusion
  489.4 105.0 %all-to-all-done.4 = bf16[32,80,1024]{2,1,0:T(8,128)(2,1)} async-done(((bf16[32,80,1024]{2,1,0:T(8,128)(2,1)}), bf16[32,80,1024]{2,1,0:T(8,128)(2,1)}, u32[]{:S(2)}, u32[]{:S(2)}) %all-to-all-start.4) | async-done | bytes 5242912 | tf_op jit(solution)/shard_map/all_to_all | solution.py:115
  599.9 6.2 fusion.24
  607.7 7.8 reduce.12
  622.5 92.9 %all-to-all-done.6 = bf16[32,80,1024]{2,1,0:T(8,128)(2,1)} async-done(((bf16[32,80,1024]{2,1,0:T(8,128)(2,1)}), bf16[32,80,1024]{2,1,0:T(8,128)(2,1)}, u32[]{:S(2)}, u32[]{:S(2)}) %all-to-all-start.6) | async-done | bytes 5242912 | tf_op jit(solution)/shard_map/all_to_all | solution.py:115
  732.8 10.2 %all-to-all-done.11 = bf16[16,2,16384]{2,1,0:T(2,128)(2,1)S(1)} async-done(((bf16[16,2,16384]{2,1,0:T(2,128)(2,1)}), bf16[16,2,16384]{2,1,0:T(2,128)(2,1)S(1)}, u32[]{:S(2)}, u32[]{:S(2)}) %all-to-all-start.11) | async-done | bytes 1048608 | tf_op jit(solution)/shard_map/all_to_all | solution.py:103
  743.0 6.9 all-to-all-start.8
  783.1 7.7 concatenate.57
  790.8 7.7 all-to-all-done.8
  802.6 5.8 reshape.484
  834.8 4.9 fusion.46
  842.4 59.5 %all-to-all-done.7 = bf16[32,32,2176]{2,1,0:T(8,128)(2,1)} async-done(((bf16[32,32,2176]{2,1,0:T(8,128)(2,1)}), bf16[32,32,2176]{2,1,0:T(8,128)(2,1)}, u32[]{:S(2)}, u32[]{:S(2)}) %all-to-all-start.7) | async-done | bytes 4456480 | tf_op jit(solution)/shard_map/all_to_all | solution.py:128
  (220 shorter events, 161.5 us)
Async XLA Ops:
  7.2 10.8 %copy-start.41 = (s32[1,2,4]{2,1,0:T(2,128)S(1)}, s32[1,2,4]{2,1,0:T(2,128)}, u32[]{:S(2)}) copy-start(s32[1,2,4]{2,1,0:T(2,128)} %param.25) | copy-start | bytes 100
  7.2 11.2 %copy-start.40 = (s32[256,8]{0,1:T(8,128)S(1)}, s32[256,8]{0,1:T(8,128)}, u32[]{:S(2)}) copy-start(s32[256,8]{0,1:T(8,128)} %param.26) | copy-start | bytes 24580
  7.2 12.1 %copy-start.11 = (bf16[256,1024]{1,0:T(8,128)(2,1)S(1)}, bf16[256,1024]{1,0:T(8,128)(2,1)}, u32[]{:S(2)}) copy-start(bf16[256,1024]{1,0:T(8,128)(2,1)} %param.14) | copy-start | bytes 1572868
  7.2 95.5 %all-gather.2.cloned.1.call-start = ((), (), s32[]{:S(2)}) async-start(), calls=%async_computation.12 | async-start | bytes 6758400 | tf_op jit(solution)/shard_map/all_gather | solution.py:164
  10.5 34.6 %all-to-all-start.1 = ((bf16[16,64,512]{2,1,0:T(8,128)(2,1)}), bf16[16,64,512]{2,1,0:T(8,128)(2,1)S(1)}, u32[]{:S(2)}, u32[]{:S(2)}) async-start(bf16[16,64,512]{2,1,0:T(8,128)(2,1)} %param.22), calls=%async_computation.1 | async-start | bytes 2097152 | tf_op jit(solution)/shard_map/all_to_all | solution.py:90
  45.1 62.6 %copy-start.17 = (bf16[16,64,512]{2,1,0:T(8,128)(2,1)}, bf16[16,64,512]{2,1,0:T(8,128)(2,1)S(1)}, u32[]{:S(2)}) copy-start(bf16[16,64,512]{2,1,0:T(8,128)(2,1)S(1)} %all-to-all-done.1) | copy-start | bytes 3145732
  45.1 65.4 %all-to-all-start.2 = ((bf16[16,64,512]{2,1,0:T(8,128)(2,1)}), bf16[16,64,512]{2,1,0:T(8,128)(2,1)}, u32[]{:S(2)}, u32[]{:S(2)}) async-start(bf16[16,64,512]{2,1,0:T(8,128)(2,1)} %param.23), calls=%async_computation.2 | async-start | bytes 2097152 | tf_op jit(solution)/shard_map/all_to_all | solution.py:90
  52.0 55.7 %copy-start.42 = (f32[256]{0:T(256)}, f32[256]{0:T(256)S(1)}, u32[]{:S(2)}) copy-start(f32[256]{0:T(256)S(1)} %add_rsqrt_fusion.1) | copy-start | bytes 3076
  104.2 18.6 %copy-start.31 = (f32[1024]{0:T(1024)}, f32[1024]{0:T(1024)S(1)}, u32[]{:S(2)}) copy-start(f32[1024]{0:T(1024)S(1)} %get-tuple-element.12) | copy-start | bytes 12292
  110.5 27.3 %all-to-all-start.3 = ((bf16[16,32,1024]{2,1,0:T(8,128)(2,1)}), bf16[16,32,1024]{2,1,0:T(8,128)(2,1)}, u32[]{:S(2)}, u32[]{:S(2)}) async-start(bf16[16,32,1024]{2,1,0:T(8,128)(2,1)} %param.24), calls=%async_computation.3 | async-start | bytes 2097152 | tf_op jit(solution)/shard_map/all_to_all | solution.py:90
  122.9 21.3 %copy-start = (bf16[256,1024]{1,0:T(8,128)(2,1)}, bf16[256,1024]{1,0:T(8,128)(2,1)S(1)}, u32[]{:S(2)}) copy-start(bf16[256,1024]{1,0:T(8,128)(2,1)S(1)} %multiply_convert_fusion.4) | copy-start | bytes 1572868
  137.8 8.6 copy-start.24
  137.8 122.6 %all-to-all-start = ((bf16[32,80,1024]{2,1,0:T(8,128)(2,1)}), bf16[32,80,1024]{2,1,0:T(8,128)(2,1)}, u32[]{:S(2)}, u32[]{:S(2)}) async-start(bf16[32,80,1024]{2,1,0:T(8,128)(2,1)} %bitcast.235), calls=%async_computation | async-start | bytes 10485760 | tf_op jit(solution)/shard_map/all_to_all | solution.py:115
  260.4 121.0 %all-to-all-start.5 = ((bf16[32,80,1024]{2,1,0:T(8,128)(2,1)}), bf16[32,80,1024]{2,1,0:T(8,128)(2,1)}, u32[]{:S(2)}, u32[]{:S(2)}) async-start(bf16[32,80,1024]{2,1,0:T(8,128)(2,1)} %multiply_convert_fusion), calls=%async_computation.5 | async-start | bytes 10485760 | tf_op jit(solution)/shard_map/all_to_all | solution.py:115
  265.3 8.1 copy-start.18
  393.4 6.3 copy-start.45
  412.5 27.8 %all-to-all-start.9 = ((bf16[16,2,16384]{2,1,0:T(2,128)(2,1)}), bf16[16,2,16384]{2,1,0:T(2,128)(2,1)}, u32[]{:S(2)}, u32[]{:S(2)}) async-start(bf16[16,2,16384]{2,1,0:T(2,128)(2,1)} %reshape.483), calls=%async_computation.9 | async-start | bytes 2097152 | tf_op jit(solution)/shard_map/all_to_all | solution.py:103
  440.3 30.1 %all-to-all-start.10 = ((bf16[16,2,16384]{2,1,0:T(2,128)(2,1)}), bf16[16,2,16384]{2,1,0:T(2,128)(2,1)S(1)}, u32[]{:S(2)}, u32[]{:S(2)}) async-start(bf16[16,2,16384]{2,1,0:T(2,128)(2,1)} %reshape.485), calls=%async_computation.10 | async-start | bytes 2097152 | tf_op jit(solution)/shard_map/all_to_all | solution.py:103
  470.4 7.9 copy-start.19
  471.4 123.0 %all-to-all-start.4 = ((bf16[32,80,1024]{2,1,0:T(8,128)(2,1)}), bf16[32,80,1024]{2,1,0:T(8,128)(2,1)}, u32[]{:S(2)}, u32[]{:S(2)}) async-start(bf16[32,80,1024]{2,1,0:T(8,128)(2,1)} %bitcast.245), calls=%async_computation.4 | async-start | bytes 10485760 | tf_op jit(solution)/shard_map/all_to_all | solution.py:115
  478.3 5.0 copy-start.46
  594.4 121.0 %all-to-all-start.6 = ((bf16[32,80,1024]{2,1,0:T(8,128)(2,1)}), bf16[32,80,1024]{2,1,0:T(8,128)(2,1)}, u32[]{:S(2)}, u32[]{:S(2)}) async-start(bf16[32,80,1024]{2,1,0:T(8,128)(2,1)} %bitcast.244), calls=%async_computation.6 | async-start | bytes 10485760 | tf_op jit(solution)/shard_map/all_to_all | solution.py:115
  715.5 27.5 %all-to-all-start.11 = ((bf16[16,2,16384]{2,1,0:T(2,128)(2,1)}), bf16[16,2,16384]{2,1,0:T(2,128)(2,1)S(1)}, u32[]{:S(2)}, u32[]{:S(2)}) async-start(bf16[16,2,16384]{2,1,0:T(2,128)(2,1)} %reshape.487), calls=%async_computation.11 | async-start | bytes 2097152 | tf_op jit(solution)/shard_map/all_to_all | solution.py:103
  743.0 10.1 %copy-start.4 = (bf16[16,2,16384]{2,1,0:T(2,128)(2,1)}, bf16[16,2,16384]{2,1,0:T(2,128)(2,1)S(1)}, u32[]{:S(2)}) copy-start(bf16[16,2,16384]{2,1,0:T(2,128)(2,1)S(1)} %all-to-all-done.11) | copy-start | bytes 3145732
  743.0 55.6 %all-to-all-start.8 = ((bf16[32,32,1024]{2,1,0:T(8,128)(2,1)}), bf16[32,32,1024]{2,1,0:T(8,128)(2,1)}, u32[]{:S(2)}, u32[]{:S(2)}) async-start(bf16[32,32,1024]{2,1,0:T(8,128)(2,1)} %bitcast.237), calls=%async_computation.8 | async-start | bytes 4194304 | tf_op jit(solution)/shard_map/all_to_all | solution.py:128
  749.9 9.1 copy-start.34
  770.9 5.5 copy-start.28
  771.1 5.3 copy-start.22
  771.8 5.7 copy-start.1
  771.8 6.4 copy-start.8
  771.8 6.4 copy-start.44
  798.6 103.3 %all-to-all-start.7 = ((bf16[32,32,2176]{2,1,0:T(8,128)(2,1)}), bf16[32,32,2176]{2,1,0:T(8,128)(2,1)}, u32[]{:S(2)}, u32[]{:S(2)}) async-start(bf16[32,32,2176]{2,1,0:T(8,128)(2,1)} %bitcast.236), calls=%async_computation.7 | async-start | bytes 8912896 | tf_op jit(solution)/shard_map/all_to_all | solution.py:128
  (28 other events, 69.3 us)
Sparse Core Ops, SparseCore 0:
  11.5 91.1 all-gather.1
where the time goes:
time: 924 us; the launch traced here: 914 us
  waiting for transfers between devices  593 us (64%)
  matrix products  126 us (14%)
  local copies, waits for them, and re-layouts  70.4 us (8%)
  starting transfers between devices  69.6 us (8%)
  other arithmetic  39.4 us (4%)
  between operations  15.5 us (2%)
    all_to_all x4, waiting for transfers between devices, exchange(): return lax.all_to_all(rows, BOTH, split_axis=0, concat_axis=0, tiled=True)  410 us
    dot_general x29, matrix products, mm(): return jnp.einsum(spec, a, b, preferred_element_type=F32)  120 us
    all_to_all x2, waiting for transfers between devices, sum_to_owners(): parts = lax.all_to_all(parts, BOTH, split_axis=0, concat_axis=0, tiled=True)  67.2 us
    all_gather x1, waiting for transfers between devices, per_device(): full = lax.all_gather(packed, BOTH, axis=0, tiled=True)  49.8 us
    all_to_all x3, waiting for transfers between devices, weight_to_expert(): lax.all_to_all(weight, 'fsdp', split_axis=0, concat_axis=1, axis_index_gr...  36.6 us
    unnamed x106, local copies, waits for them, and re-layouts  35.7 us
    all_to_all x3, waiting for transfers between devices, grad_to_owners(): lax.all_to_all(grad.astype(BF16)[None], 'fsdp', split_axis=1, concat_axis...  30.2 us
    unnamed x4, other arithmetic  23.9 us
  transfers between devices with their start and end apart: 13, of which 12 were waited for; matrix products, arithmetic and copies ran while one was open for 21% of the time, Pallas kernels for 0%

commit v1 on v0

--- a/solution.py
+++ b/solution.py
@@ -24,6 +24,18 @@
 BOTH = ("fsdp", "expert")
 F32 = jnp.float32
 BF16 = jnp.bfloat16
+
+
+def collect(x, axis, dim):
+    ways, here = (lax.axis_size(axis), lax.axis_index(axis))
+    grown, reach = (x, 1)
+    while reach < ways:
+        theirs = lax.ppermute(grown, axis, [(d, d ^ reach) for d in range(ways)])
+        mine_first = jnp.concatenate([grown, theirs], axis=dim)
+        theirs_first = jnp.concatenate([theirs, grown], axis=dim)
+        grown = jnp.where(here & reach == 0, mine_first, theirs_first)
+        reach = 2 * reach
+    return grown
 
 
 def mm(spec, a, b):
@@ -161,7 +173,7 @@
     packed = jnp.concatenate(
         [query_weight, key_projection, value_projection, output_weight, small], axis=1
     )
-    full = lax.all_gather(packed, BOTH, axis=0, tiled=True)
+    full = collect(packed, BOTH, 0)
     qkv_full = full[:, :QKV_COLS]
     o_full = full[:, QKV_COLS : QKV_COLS + MODEL_WIDTH]
     small_full = full[:, QKV_COLS + MODEL_WIDTH :]

time: 924 us -> 1080 us (1.17)
  waiting for transfers between devices: 593 us -> 742 us
  between operations: 15.5 us -> 1.9 us
  starting transfers between devices: 69.6 us -> 82.4 us
    all_to_all x3, waiting for transfers between devices: 36.6 us -> 174 us  [weight_to_expert(): lax.all_to_all(weight, 'fsdp', split_axis=0, concat_axis=1, axis_index_gr...]
    ppermute x0 -> x5, waiting for transfers between devices: none -> 60.7 us  [collect(): theirs = lax.ppermute(grown, axis, [(d, d ^ reach) for d in range(ways)])]
    all_gather x1 -> x0, waiting for transfers between devices: 49.8 us -> none  [per_device(): full = lax.all_gather(packed, BOTH, axis=0, tiled=True)]
    unnamed x106 -> x104, local copies, waits for them, and re-layouts: 35.7 us -> 29.9 us
  transfers between devices with their start and end apart: 13 -> 17, of which waited for: 12 -> 16; matrix products, arithmetic and copies ran while one was open for 21% -> 18% of each run, Pallas kernels for 0% -> 0%
where the time goes in v1:
time: 1080 us; the launch traced here: 1070 us
  waiting for transfers between devices  742 us (69%)
  matrix products  126 us (12%)
  starting transfers between devices  82.4 us (8%)
  local copies, waits for them, and re-layouts  67.3 us (6%)
  other arithmetic  49.3 us (5%)
    all_to_all x4, waiting for transfers between devices, exchange(): return lax.all_to_all(rows, BOTH, split_axis=0, concat_axis=0, tiled=True)  408 us
    all_to_all x3, waiting for transfers between devices, weight_to_expert(): lax.all_to_all(weight, 'fsdp', split_axis=0, concat_axis=1, axis_index_gr...  174 us
    dot_general x29, matrix products, mm(): return jnp.einsum(spec, a, b, preferred_element_type=F32)  121 us
    all_to_all x2, waiting for transfers between devices, sum_to_owners(): parts = lax.all_to_all(parts, BOTH, split_axis=0, concat_axis=0, tiled=True)  69.3 us
    ppermute x5, waiting for transfers between devices, collect(): theirs = lax.ppermute(grown, axis, [(d, d ^ reach) for d in range(ways)])  60.7 us
    unnamed x104, local copies, waits for them, and re-layouts  29.9 us
    all_to_all x3, waiting for transfers between devices, grad_to_owners(): lax.all_to_all(grad.astype(BF16)[None], 'fsdp', split_axis=1, concat_axis...  29.9 us
    unnamed x4, other arithmetic  24.2 us
  transfers between devices with their start and end apart: 17, of which 16 were waited for; matrix products, arithmetic and copies ran while one was open for 18% of the time, Pallas kernels for 0%

profile of v1, /device:TPU:0, one launch (start us, length us, event | category | flops | bytes accessed | tf_op | source)
XLA Modules:
  0.0 1068.8 jit_solution(798814477755803466)
XLA Ops:
  15.1 18.5 %collective-permute-done.2 = bf16[128,3200]{1,0:T(8,128)(2,1)S(1)} collective-permute-done((bf16[128,3200]{1,0:T(8,128)(2,1)S(1)}, bf16[128,3200]{1,0:T(8,128)(2,1)S(1)}, u32[]{:S(2)}, u32[]{:S(2)}) %collective-permute-start.2) | collective-permute-done | bytes 819232 | tf_op jit(solution)/shard_map/ppermute | solution.py:33
  35.9 35.3 %collective-permute-done.3 = bf16[256,3200]{1,0:T(8,128)(2,1)} collective-permute-done((bf16[256,3200]{1,0:T(8,128)(2,1)S(1)}, bf16[256,3200]{1,0:T(8,128)(2,1)}, u32[]{:S(2)}, u32[]{:S(2)}) %collective-permute-start.3) | collective-permute-done | bytes 1638432 | tf_op jit(solution)/shard_map/ppermute | solution.py:33
  85.7 149.9 %all-to-all-done.1 = bf16[16,64,512]{2,1,0:T(8,128)(2,1)} async-done(((bf16[16,64,512]{2,1,0:T(8,128)(2,1)}), bf16[16,64,512]{2,1,0:T(8,128)(2,1)}, u32[]{:S(2)}, u32[]{:S(2)}) %all-to-all-start.1) | async-done | bytes 1048608 | tf_op jit(solution)/shard_map/all_to_all | solution.py:102
  235.5 10.1 all-to-all-start.2
  257.1 11.5 %all-to-all-done.2 = bf16[16,64,512]{2,1,0:T(8,128)(2,1)} async-done(((bf16[16,64,512]{2,1,0:T(8,128)(2,1)}), bf16[16,64,512]{2,1,0:T(8,128)(2,1)}, u32[]{:S(2)}, u32[]{:S(2)}) %all-to-all-start.2) | async-done | bytes 1048608 | tf_op jit(solution)/shard_map/all_to_all | solution.py:102
  268.5 6.8 all-to-all-start.3
  285.7 12.6 %all-to-all-done.3 = bf16[16,32,1024]{2,1,0:T(8,128)(2,1)} async-done(((bf16[16,32,1024]{2,1,0:T(8,128)(2,1)}), bf16[16,32,1024]{2,1,0:T(8,128)(2,1)}, u32[]{:S(2)}, u32[]{:S(2)}) %all-to-all-start.3) | async-done | bytes 1048608 | tf_op jit(solution)/shard_map/all_to_all | solution.py:102
  298.3 7.0 all-to-all-start
  310.7 110.7 %all-to-all-done = bf16[32,80,1024]{2,1,0:T(8,128)(2,1)} async-done(((bf16[32,80,1024]{2,1,0:T(8,128)(2,1)}), bf16[32,80,1024]{2,1,0:T(8,128)(2,1)}, u32[]{:S(2)}, u32[]{:S(2)}) %all-to-all-start) | async-done | bytes 5242912 | tf_op jit(solution)/shard_map/all_to_all | solution.py:127
  426.2 8.0 fusion.120
  434.2 8.0 fusion.119
  442.2 100.1 %all-to-all-done.5 = bf16[32,80,1024]{2,1,0:T(8,128)(2,1)} async-done(((bf16[32,80,1024]{2,1,0:T(8,128)(2,1)}), bf16[32,80,1024]{2,1,0:T(8,128)(2,1)}, u32[]{:S(2)}, u32[]{:S(2)}) %all-to-all-start.5) | async-done | bytes 5242912 | tf_op jit(solution)/shard_map/all_to_all | solution.py:127
  542.3 12.2 %multiply_convert_fusion.1 = (bf16[2560,512]{1,0:T(8,128)(2,1)}, bf16[2560,512]{1,0:T(8,128)(2,1)S(1)}, bf16[2560,512]{1,0:T(8,128)(2,1)}) fusion(f32[2560,512]{1,0:T(8,128)} %fusion.119, f32[2560,512]{1,0:T(8,128)} %fusion.120, bf16[2560,1024]{1,0:T(8,128)(2,1)} %bitcast.37, bf16[512,1024]{1,0:T(8,128)(2,1)} %bitcast.26), kind=kOutput, calls=%fused_computation.7 | convolution fusion | flops 2704015360 | bytes 24641536 | tf_op jit(solution)/shard_map/sd,hd->sh/dot_general | solution.py:42
  554.5 6.3 fusion.22
  564.3 8.0 reduce.10
  579.0 6.2 fusion.23
  588.1 8.0 reduce.11
  601.9 7.0 all-to-all-start.10
  608.8 7.2 convolution_convert_fusion.1
  616.1 15.6 %all-to-all-done.10 = bf16[16,2,16384]{2,1,0:T(2,128)(2,1)S(1)} async-done(((bf16[16,2,16384]{2,1,0:T(2,128)(2,1)}), bf16[16,2,16384]{2,1,0:T(2,128)(2,1)S(1)}, u32[]{:S(2)}, u32[]{:S(2)}) %all-to-all-start.10) | async-done | bytes 1048608 | tf_op jit(solution)/shard_map/all_to_all | solution.py:115
  632.7 6.9 all-to-all-start.4
  639.6 5.3 fusion.121
  644.9 6.0 add_convert_fusion
  650.9 104.8 %all-to-all-done.4 = bf16[32,80,1024]{2,1,0:T(8,128)(2,1)} async-done(((bf16[32,80,1024]{2,1,0:T(8,128)(2,1)}), bf16[32,80,1024]{2,1,0:T(8,128)(2,1)}, u32[]{:S(2)}, u32[]{:S(2)}) %all-to-all-start.4) | async-done | bytes 5242912 | tf_op jit(solution)/shard_map/all_to_all | solution.py:127
  761.3 6.2 fusion.24
  770.4 8.1 reduce.12
  784.2 92.5 %all-to-all-done.6 = bf16[32,80,1024]{2,1,0:T(8,128)(2,1)} async-done(((bf16[32,80,1024]{2,1,0:T(8,128)(2,1)}), bf16[32,80,1024]{2,1,0:T(8,128)(2,1)}, u32[]{:S(2)}, u32[]{:S(2)}) %all-to-all-start.6) | async-done | bytes 5242912 | tf_op jit(solution)/shard_map/all_to_all | solution.py:127
  894.6 10.1 all-to-all-done.11
  904.7 6.9 all-to-all-start.8
  945.0 7.8 concatenate.97
  952.7 7.5 all-to-all-done.8
  1001.7 61.8 %all-to-all-done.7 = bf16[32,32,2176]{2,1,0:T(8,128)(2,1)} async-done(((bf16[32,32,2176]{2,1,0:T(8,128)(2,1)}), bf16[32,32,2176]{2,1,0:T(8,128)(2,1)}, u32[]{:S(2)}, u32[]{:S(2)}) %all-to-all-start.7) | async-done | bytes 4456480 | tf_op jit(solution)/shard_map/all_to_all | solution.py:140
  (230 shorter events, 193.8 us)
Async XLA Ops:
  3.1 8.1 collective-permute-start
  11.3 1.8 collective-permute-start.1
  13.3 20.4 %collective-permute-start.2 = (bf16[128,3200]{1,0:T(8,128)(2,1)S(1)}, bf16[128,3200]{1,0:T(8,128)(2,1)S(1)}, u32[]{:S(2)}, u32[]{:S(2)}) collective-permute-start(bf16[128,3200]{1,0:T(8,128)(2,1)S(1)} %maximum_select_fusion.3), channel_id=1, source_target_pairs={{0,4},{1,5},{2,6},{3,7},{4,0},{5,1},{6,2},{7,3},{8,12},{9,13},{10,... | collective-permute-start | bytes 2457608 | tf_op jit(solution)/shard_map/ppermute | solution.py:33
  34.0 37.2 %collective-permute-start.3 = (bf16[256,3200]{1,0:T(8,128)(2,1)S(1)}, bf16[256,3200]{1,0:T(8,128)(2,1)}, u32[]{:S(2)}, u32[]{:S(2)}) collective-permute-start(bf16[256,3200]{1,0:T(8,128)(2,1)S(1)} %maximum_select_fusion.2), channel_id=1, source_target_pairs={{0,8},{1,9},{2,10},{3,11},{4,12},{5,13},{6,14},{7,15},{8,0},{9,1},... | collective-permute-start | bytes 4915208 | tf_op jit(solution)/shard_map/ppermute | solution.py:33
  35.8 46.0 %copy-start.39 = (s32[256,8]{0,1:T(8,128)S(1)}, s32[256,8]{0,1:T(8,128)}, u32[]{:S(2)}) copy-start(s32[256,8]{0,1:T(8,128)} %param.26) | copy-start | bytes 24580
  35.8 46.2 %copy-start.40 = (s32[1,2,4]{2,1,0:T(2,128)S(1)}, s32[1,2,4]{2,1,0:T(2,128)}, u32[]{:S(2)}) copy-start(s32[1,2,4]{2,1,0:T(2,128)} %param.25) | copy-start | bytes 100
  74.7 170.9 %collective-permute-start.4 = (bf16[512,3200]{1,0:T(8,128)(2,1)S(1)}, bf16[512,3200]{1,0:T(8,128)(2,1)}, u32[]{:S(2)}, u32[]{:S(2)}) collective-permute-start(bf16[512,3200]{1,0:T(8,128)(2,1)S(1)} %maximum_select_fusion.1), channel_id=1, source_target_pairs={{0,16},{1,17},{2,18},{3,19},{4,20},{5,21},{6,22},{7,23},{8,24},{9,... | collective-permute-start | bytes 9830408 | tf_op jit(solution)/shard_map/ppermute | solution.py:33
  77.5 158.0 %all-to-all-start.1 = ((bf16[16,64,512]{2,1,0:T(8,128)(2,1)}), bf16[16,64,512]{2,1,0:T(8,128)(2,1)}, u32[]{:S(2)}, u32[]{:S(2)}) async-start(bf16[16,64,512]{2,1,0:T(8,128)(2,1)} %param.22), calls=%async_computation.1 | async-start | bytes 2097152 | tf_op jit(solution)/shard_map/all_to_all | solution.py:102
  85.3 165.9 %copy-start.41 = (f32[256]{0:T(256)}, f32[256]{0:T(256)S(1)}, u32[]{:S(2)}) copy-start(f32[256]{0:T(256)S(1)} %add_rsqrt_fusion.1) | copy-start | bytes 3076
  235.5 33.0 %all-to-all-start.2 = ((bf16[16,64,512]{2,1,0:T(8,128)(2,1)}), bf16[16,64,512]{2,1,0:T(8,128)(2,1)}, u32[]{:S(2)}, u32[]{:S(2)}) async-start(bf16[16,64,512]{2,1,0:T(8,128)(2,1)} %param.23), calls=%async_computation.2 | async-start | bytes 2097152 | tf_op jit(solution)/shard_map/all_to_all | solution.py:102
  245.6 8.0 copy-start.16
  268.5 29.8 %all-to-all-start.3 = ((bf16[16,32,1024]{2,1,0:T(8,128)(2,1)}), bf16[16,32,1024]{2,1,0:T(8,128)(2,1)}, u32[]{:S(2)}, u32[]{:S(2)}) async-start(bf16[16,32,1024]{2,1,0:T(8,128)(2,1)} %param.24), calls=%async_computation.3 | async-start | bytes 2097152 | tf_op jit(solution)/shard_map/all_to_all | solution.py:102
  281.9 23.4 %copy-start.1 = (bf16[256,1024]{1,0:T(8,128)(2,1)}, bf16[256,1024]{1,0:T(8,128)(2,1)S(1)}, u32[]{:S(2)}) copy-start(bf16[256,1024]{1,0:T(8,128)(2,1)S(1)} %multiply_convert_fusion.4) | copy-start | bytes 1572868
  298.3 9.1 copy-start.23
  298.3 123.1 %all-to-all-start = ((bf16[32,80,1024]{2,1,0:T(8,128)(2,1)}), bf16[32,80,1024]{2,1,0:T(8,128)(2,1)}, u32[]{:S(2)}, u32[]{:S(2)}) async-start(bf16[32,80,1024]{2,1,0:T(8,128)(2,1)} %bitcast.235), calls=%async_computation | async-start | bytes 10485760 | tf_op jit(solution)/shard_map/all_to_all | solution.py:127
  421.4 120.9 %all-to-all-start.5 = ((bf16[32,80,1024]{2,1,0:T(8,128)(2,1)}), bf16[32,80,1024]{2,1,0:T(8,128)(2,1)}, u32[]{:S(2)}, u32[]{:S(2)}) async-start(bf16[32,80,1024]{2,1,0:T(8,128)(2,1)} %multiply_convert_fusion), calls=%async_computation.5 | async-start | bytes 10485760 | tf_op jit(solution)/shard_map/all_to_all | solution.py:127
  554.5 6.3 copy-start.44
  573.9 27.9 %all-to-all-start.9 = ((bf16[16,2,16384]{2,1,0:T(2,128)(2,1)}), bf16[16,2,16384]{2,1,0:T(2,128)(2,1)S(1)}, u32[]{:S(2)}, u32[]{:S(2)}) async-start(bf16[16,2,16384]{2,1,0:T(2,128)(2,1)} %reshape.483), calls=%async_computation.9 | async-start | bytes 2097152 | tf_op jit(solution)/shard_map/all_to_all | solution.py:115
  601.9 14.2 %copy-start.4 = (bf16[16,2,16384]{2,1,0:T(2,128)(2,1)}, bf16[16,2,16384]{2,1,0:T(2,128)(2,1)S(1)}, u32[]{:S(2)}) copy-start(bf16[16,2,16384]{2,1,0:T(2,128)(2,1)S(1)} %all-to-all-done.9) | copy-start | bytes 3145732
  601.9 29.8 %all-to-all-start.10 = ((bf16[16,2,16384]{2,1,0:T(2,128)(2,1)}), bf16[16,2,16384]{2,1,0:T(2,128)(2,1)S(1)}, u32[]{:S(2)}, u32[]{:S(2)}) async-start(bf16[16,2,16384]{2,1,0:T(2,128)(2,1)} %reshape.485), calls=%async_computation.10 | async-start | bytes 2097152 | tf_op jit(solution)/shard_map/all_to_all | solution.py:115
  632.7 123.0 %all-to-all-start.4 = ((bf16[32,80,1024]{2,1,0:T(8,128)(2,1)}), bf16[32,80,1024]{2,1,0:T(8,128)(2,1)}, u32[]{:S(2)}, u32[]{:S(2)}) async-start(bf16[32,80,1024]{2,1,0:T(8,128)(2,1)} %bitcast.245), calls=%async_computation.4 | async-start | bytes 10485760 | tf_op jit(solution)/shard_map/all_to_all | solution.py:127
  639.6 5.3 copy-start.45
  755.7 121.1 %all-to-all-start.6 = ((bf16[32,80,1024]{2,1,0:T(8,128)(2,1)}), bf16[32,80,1024]{2,1,0:T(8,128)(2,1)}, u32[]{:S(2)}, u32[]{:S(2)}) async-start(bf16[32,80,1024]{2,1,0:T(8,128)(2,1)} %bitcast.244), calls=%async_computation.6 | async-start | bytes 10485760 | tf_op jit(solution)/shard_map/all_to_all | solution.py:127
  770.4 9.7 copy-start.24
  876.8 27.9 %all-to-all-start.11 = ((bf16[16,2,16384]{2,1,0:T(2,128)(2,1)}), bf16[16,2,16384]{2,1,0:T(2,128)(2,1)S(1)}, u32[]{:S(2)}, u32[]{:S(2)}) async-start(bf16[16,2,16384]{2,1,0:T(2,128)(2,1)} %reshape.487), calls=%async_computation.11 | async-start | bytes 2097152 | tf_op jit(solution)/shard_map/all_to_all | solution.py:115
  904.7 10.1 copy-start.8
  904.7 55.6 %all-to-all-start.8 = ((bf16[32,32,1024]{2,1,0:T(8,128)(2,1)}), bf16[32,32,1024]{2,1,0:T(8,128)(2,1)}, u32[]{:S(2)}, u32[]{:S(2)}) async-start(bf16[32,32,1024]{2,1,0:T(8,128)(2,1)} %bitcast.237), calls=%async_computation.8 | async-start | bytes 4194304 | tf_op jit(solution)/shard_map/all_to_all | solution.py:140
  932.1 5.0 copy-start.28
  932.3 5.8 copy-start.2
  932.4 6.5 copy-start.13
  932.4 6.5 copy-start.43
  960.3 103.2 %all-to-all-start.7 = ((bf16[32,32,2176]{2,1,0:T(8,128)(2,1)}), bf16[32,32,2176]{2,1,0:T(8,128)(2,1)}, u32[]{:S(2)}, u32[]{:S(2)}) async-start(bf16[32,32,2176]{2,1,0:T(8,128)(2,1)} %bitcast.236), calls=%async_computation.7 | async-start | bytes 8912896 | tf_op jit(solution)/shard_map/all_to_all | solution.py:140
  (31 other events, 92.9 us)
